TPU v7x, 512 devices: a whole 4x4x16 slice. The times are simulated.
512 devices in a mesh: ctx: 32 (over x_hi, z), fsdp: 16 (over y, x_lo, core).
Axes of the slice: x: 4 (x_hi: 2, x_lo: 2; x = x_hi * 2 + x_lo), y: 4, z: 16, core: 2. Of those that a mesh axis runs over, the one named last changes fastest.
Arguments:
- streams: bfloat16 [3, 16384, 8192], P(None, ('ctx', 'fsdp')), may hold values from -6 to 6
- segments: int32 [16384], replicated, may hold values from 0 to 63, never falling along the last dimension, each value on 1 to 4096 neighbouring positions
- short_taps: float32 [3, 3, 8192], P(None, None, 'fsdp'), may hold values from -3 to 3
- decay_rates: float32 [512, 16], P('fsdp'), may hold values from 1.2207031e-05 to 0.1
- residues: float32 [512, 16], P('fsdp'), may hold values from -2 to 2
- skip_gain: float32 [8192], P('fsdp'), may hold values from -4 to 4
Outputs:
- output: bfloat16 [16384, 8192], P(('ctx', 'fsdp'))
Inputs may be any that keep to these rules, and one draw needn't show every extreme that they name: `segments`: never falling along the window; every document has 1 to 4096 tokens and one has exactly 4096.
All inputs are finite; a program needn't handle non-finite values.
Results may differ from a plain program's by a relative error of at most 0.0064.
Values may be sent and summed in bfloat16 or wider, within the bound.
A program may use at most 64 MiB of HBM per device.

v0:
```python
import jax
import jax.numpy as jnp
from jax import lax
from jax.sharding import PartitionSpec as P

GROUP = 16
MODES = 16
SHORT = 3
SPAN = 8


def shifted_2(block, axis, distance):
    devices = range(lax.axis_size(axis))
    route = [(i - distance, i) for i in devices if i - distance in devices]
    return lax.ppermute(block, axis, route)


def contract(pattern, left_side, right_side):
    return jnp.einsum(pattern, left_side, right_side, precision=lax.Precision.HIGHEST)


def featurize(block_rows, before_rows, tap_rows, row_marks, before_marks):
    margin = before_rows.shape[1]
    row_count = block_rows.shape[1]
    joined = jnp.concatenate([before_rows, block_rows], axis=1)
    all_marks = jnp.concatenate([before_marks, row_marks])
    summed = block_rows.astype(jnp.float32) * tap_rows[:, 0][:, None, :]
    for offset in range(1, margin + 1):
        shifted = joined[:, margin - offset : margin - offset + row_count].astype(jnp.float32)
        agreeing = all_marks[margin - offset : margin - offset + row_count] == row_marks
        summed = (
            summed
            + jnp.where(agreeing[None, :, None], shifted, 0.0) * tap_rows[:, offset][:, None, :]
        )
    queries = summed[0].astype(jnp.bfloat16)
    gated_prod = (summed[1] * summed[2]).astype(jnp.bfloat16)
    return lax.optimization_barrier((queries, gated_prod))


def tile_filter(gated_prod, tile_marks, decay_rates, mode_gain, rising):
    tile_rows, channels = gated_prod.shape
    groups = channels // GROUP
    block_len = min(128, tile_rows)
    offsets = jnp.arange(block_len, dtype=jnp.float32)
    forward = mode_gain[:, :, None] * jnp.exp(-decay_rates[:, :, None] * offsets)
    backward = jnp.exp(decay_rates[:, :, None] * offsets)
    causal = (offsets[:, None] >= offsets[None, :]).astype(jnp.float32)
    kernel = contract("gmt,gms->gts", forward, backward) * causal
    mode_rates = decay_rates.T[:, :, None]
    closing = jnp.exp(-mode_rates * (block_len - 1.0 - offsets))
    through = jnp.exp(-mode_rates * block_len)
    head_rising = rising[:, :, :block_len]
    values = gated_prod.astype(jnp.float32).reshape(tile_rows, groups, GROUP)
    carried = jnp.zeros((MODES, groups, GROUP), jnp.float32)
    last_seen = jnp.int32(-1)
    pieces = []
    for number in range(tile_rows // block_len):
        block_vals = values[number * block_len : (number + 1) * block_len]
        block_marks = tile_marks[number * block_len : (number + 1) * block_len]
        agreeing = (block_marks[:, None] == block_marks[None, :]).astype(jnp.float32)
        inside = contract("gts,sgc->tgc", kernel * agreeing, block_vals)
        follow = (block_marks == last_seen).astype(jnp.float32)
        inside = inside + follow[:, None, None] * contract("mgt,mgc->tgc", head_rising, carried)
        ending = (block_marks == block_marks[block_len - 1]).astype(jnp.float32)
        fresh_state = contract("mgs,sgc->mgc", closing * ending, block_vals)
        passing = (block_marks[block_len - 1] == last_seen).astype(jnp.float32)
        carried = fresh_state + passing * through * carried
        last_seen = block_marks[block_len - 1]
        pieces.append(inside)
    return (jnp.concatenate(pieces, axis=0), carried)


def local(streams, segments, short_taps, decay_rates, residues, skip_gain):
    fsdp_count = lax.axis_size("fsdp")
    ctx_count = lax.axis_size("ctx")
    tile_index = lax.axis_index("ctx")
    own_rows = streams.shape[1]
    tile_rows = own_rows * fsdp_count
    margin = SHORT - 1
    padded_marks = jnp.concatenate([jnp.full((margin,), -1, jnp.int32), segments])
    tile_start = tile_index * tile_rows
    tile_marks = lax.dynamic_slice_in_dim(segments, tile_start, tile_rows)
    local_streams = lax.all_to_all(streams, "fsdp", split_axis=2, concat_axis=1, tiled=True)
    before_rows = shifted_2(local_streams[:, tile_rows - margin :, :], "ctx", 1)
    before_marks = lax.dynamic_slice_in_dim(padded_marks, tile_start, margin)
    queries, gated_prod = featurize(
        local_streams, before_rows, short_taps, tile_marks, before_marks
    )
    channels = gated_prod.shape[1]
    groups = channels // GROUP
    mode_gain = residues * jnp.sqrt(-jnp.expm1(-2.0 * decay_rates))
    positions = jnp.arange(tile_rows, dtype=jnp.float32)
    mode_rates = decay_rates.T[:, :, None]
    rising = mode_gain.T[:, :, None] * jnp.exp(-mode_rates * (positions + 1.0))
    local_part, end_state = tile_filter(gated_prod, tile_marks, decay_rates, mode_gain, rising)
    first_mark = tile_marks[0]
    falling = jnp.exp(-mode_rates * (tile_rows - 1.0 - positions))

    def source_state(operand):
        source_vals, source_marks = operand
        chosen = (source_marks == first_mark).astype(jnp.float32)
        return contract(
            "mgs,sgc->mgc",
            falling * chosen,
            source_vals.astype(jnp.float32).reshape(tile_rows, groups, GROUP),
        )

    def empty_state(operand):
        return jnp.zeros((MODES, groups, GROUP), jnp.float32)

    prior_state = jnp.zeros((MODES, groups, GROUP), jnp.float32)
    for distance in range(1, min(SPAN, ctx_count - 1) + 1):
        source_tile = shifted_2(gated_prod, "ctx", distance)
        source_index = tile_index - distance
        source_marks = lax.dynamic_slice_in_dim(
            segments, jnp.maximum(source_index, 0) * tile_rows, tile_rows
        )
        paired = (source_index >= 0) & (source_marks[tile_rows - 1] == first_mark)
        received = lax.cond(paired, source_state, empty_state, (source_tile, source_marks))
        prior_state = prior_state + jnp.exp(-mode_rates * ((distance - 1) * tile_rows)) * received
    prior_mark = first_mark.astype(jnp.float32)
    follow_tile = (tile_marks.astype(jnp.float32) == prior_mark).astype(jnp.float32)
    filtered = local_part + follow_tile[:, None, None] * contract(
        "mgt,mgc->tgc", rising, prior_state
    )
    mixed_out = (
        filtered.reshape(tile_rows, channels) + skip_gain * gated_prod.astype(jnp.float32)
    ).astype(jnp.bfloat16)
    mixed_out = lax.optimization_barrier(mixed_out)
    payload = (queries.astype(jnp.float32) * mixed_out.astype(jnp.float32)).astype(jnp.bfloat16)
    returned = lax.all_to_all(payload, "fsdp", split_axis=0, concat_axis=1, tiled=True)
    return returned


def solution(mesh):
    placed = (
        P(None, ("ctx", "fsdp"), None),
        P(),
        P(None, None, "fsdp"),
        P("fsdp", None),
        P("fsdp", None),
        P("fsdp"),
    )
    return jax.shard_map(
        local, mesh=mesh, in_specs=placed, out_specs=P(("ctx", "fsdp"), None), check_vma=False
    )
```

profile of v0, /device:TPU:4, one launch (start us, length us, event | category | flops | bytes accessed | tf_op | source)
XLA Modules:
  0.0 510.9 jit_solution(597949325799028393)
XLA Ops:
  0.0 10.6 %copy.91 = bf16[3,32,8192]{1,0,2:T(4,128)(2,1)} copy(bf16[3,32,8192]{2,1,0:T(8,128)(2,1)} %param.22) | data formatting | bytes 3145728 | tf_op args[0]
  10.6 13.2 %reshape.234 = bf16[16,2,24576]{2,1,0:T(2,128)(2,1)} reshape(bf16[8192,3,32]{2,1,0:T(4,128)(2,1)} %bitcast.120) | data formatting | bytes 3145728
  23.8 5.4 %all-to-all-start = ((bf16[16,2,24576]{2,1,0:T(2,128)(2,1)}), bf16[16,2,24576]{2,1,0:T(2,128)(2,1)}, u32[]{:S(2)}, u32[]{:S(2)}) async-start(bf16[16,2,24576]{2,1,0:T(2,128)(2,1)} %reshape.234), calls=%async_computation | async-start | bytes 3145728 | tf_op jit(solution)/shard_map/all_to_all | solution.py:83
  33.3 2.5 compare_convert_fusion.18
  41.6 3.7 fusion.87
  45.3 6.2 %all-to-all-done = bf16[16,2,24576]{2,1,0:T(2,128)(2,1)} async-done(((bf16[16,2,24576]{2,1,0:T(2,128)(2,1)}), bf16[16,2,24576]{2,1,0:T(2,128)(2,1)}, u32[]{:S(2)}, u32[]{:S(2)}) %all-to-all-start) | async-done | bytes 1572896 | tf_op jit(solution)/shard_map/all_to_all | solution.py:83
  51.5 12.6 %reshape.235 = bf16[8192,3,32]{2,1,0:T(4,128)(2,1)} reshape(bf16[16,2,24576]{2,1,0:T(2,128)(2,1)} %all-to-all-done) | data formatting | bytes 3145728
  64.1 11.8 %copy.128 = bf16[3,32,16,512]{3,1,2,0:T(8,128)(2,1)} copy(bf16[3,32,16,512]{1,0,3,2:T(4,128)(2,1)} %bitcast.119) | data formatting | bytes 3145728 | tf_op jit(solution)/shard_map/all_to_all | solution.py:83
  76.6 3.8 collective-permute-start
  103.3 3.9 multiply_add_fusion
  110.8 14.8 %collective-permute-start.8 = (bf16[512,512]{1,0:T(8,128)(2,1)}, bf16[512,512]{1,0:T(8,128)(2,1)}, u32[]{:S(2)}, u32[]{:S(2)}) collective-permute-start(bf16[512,512]{1,0:T(8,128)(2,1)} %fusion.68), channel_id=1, source_target_pairs={{0,128},{16,144},{32,160},{48,176},{64,192},{80,208},{96,224},{112... | collective-permute-start | bytes 1572872 | tf_op jit(solution)/shard_map/ppermute | solution.py:15
  125.7 4.0 collective-permute-start.7
  129.7 3.1 collective-permute-start.6
  151.7 2.5 fusion.34
  154.2 13.2 %collective-permute-start.3 = (bf16[512,512]{1,0:T(8,128)(2,1)}, bf16[512,512]{1,0:T(8,128)(2,1)}, u32[]{:S(2)}, u32[]{:S(2)}) collective-permute-start(bf16[512,512]{1,0:T(8,128)(2,1)} %fusion.68), channel_id=1, source_target_pairs={{0,48},{16,64},{32,80},{48,96},{64,112},{80,128},{96,144},{112,160... | collective-permute-start | bytes 1572872 | tf_op jit(solution)/shard_map/ppermute | solution.py:15
  167.4 104.7 %collective-permute-done.7 = bf16[512,512]{1,0:T(8,128)(2,1)} collective-permute-done((bf16[512,512]{1,0:T(8,128)(2,1)}, bf16[512,512]{1,0:T(8,128)(2,1)}, u32[]{:S(2)}, u32[]{:S(2)}) %collective-permute-start.7) | collective-permute-done | bytes 524320 | tf_op jit(solution)/shard_map/ppermute | solution.py:15
  272.0 17.1 %collective-permute-start.2 = (bf16[512,512]{1,0:T(8,128)(2,1)}, bf16[512,512]{1,0:T(8,128)(2,1)}, u32[]{:S(2)}, u32[]{:S(2)}) collective-permute-start(bf16[512,512]{1,0:T(8,128)(2,1)} %fusion.68), channel_id=1, source_target_pairs={{0,32},{16,48},{32,64},{48,80},{64,96},{80,112},{96,128},{112,144}... | collective-permute-start | bytes 1572872 | tf_op jit(solution)/shard_map/ppermute | solution.py:15
  289.2 59.7 %collective-permute-done.6 = bf16[512,512]{1,0:T(8,128)(2,1)} collective-permute-done((bf16[512,512]{1,0:T(8,128)(2,1)}, bf16[512,512]{1,0:T(8,128)(2,1)}, u32[]{:S(2)}, u32[]{:S(2)}) %collective-permute-start.6) | collective-permute-done | bytes 524320 | tf_op jit(solution)/shard_map/ppermute | solution.py:15
  351.2 2.5 fusion.52
  354.3 2.6 conditional.14
  357.0 2.6 conditional.13
  359.6 2.7 conditional.12
  362.3 73.8 %collective-permute-done.4 = bf16[512,512]{1,0:T(8,128)(2,1)} collective-permute-done((bf16[512,512]{1,0:T(8,128)(2,1)}, bf16[512,512]{1,0:T(8,128)(2,1)}, u32[]{:S(2)}, u32[]{:S(2)}) %collective-permute-start.4) | collective-permute-done | bytes 524320 | tf_op jit(solution)/shard_map/ppermute | solution.py:15
  436.2 2.6 conditional.11
  438.8 14.5 %collective-permute-done.3 = bf16[512,512]{1,0:T(8,128)(2,1)} collective-permute-done((bf16[512,512]{1,0:T(8,128)(2,1)}, bf16[512,512]{1,0:T(8,128)(2,1)}, u32[]{:S(2)}, u32[]{:S(2)}) %collective-permute-start.3) | collective-permute-done | bytes 524320 | tf_op jit(solution)/shard_map/ppermute | solution.py:15
  453.4 2.6 conditional.10
  455.9 18.9 %collective-permute-done.2 = bf16[512,512]{1,0:T(8,128)(2,1)} collective-permute-done((bf16[512,512]{1,0:T(8,128)(2,1)}, bf16[512,512]{1,0:T(8,128)(2,1)}, u32[]{:S(2)}, u32[]{:S(2)}) %collective-permute-start.2) | collective-permute-done | bytes 524320 | tf_op jit(solution)/shard_map/ppermute | solution.py:15
  474.8 2.6 conditional.9
  477.5 8.3 %collective-permute-done.1 = bf16[512,512]{1,0:T(8,128)(2,1)} collective-permute-done((bf16[512,512]{1,0:T(8,128)(2,1)}, bf16[512,512]{1,0:T(8,128)(2,1)}, u32[]{:S(2)}, u32[]{:S(2)}) %collective-permute-start.1) | collective-permute-done | bytes 524320 | tf_op jit(solution)/shard_map/ppermute | solution.py:15
  485.9 4.0 conditional.8
  490.0 3.3 fusion.30
  495.3 14.7 %all_to_all.37 = bf16[16,32,512]{2,1,0:T(8,128)(2,1)S(1)} all-to-all(bf16[16,32,512]{2,1,0:T(8,128)(2,1)S(1)} %bitcast.124), channel_id=1, replica_groups=mesh['ctx'=32,'fsdp'=16] {'fsdp'}, dimensions={0} | all-to-all | bytes 1048576 | tf_op jit(solution)/shard_map/all_to_all | solution.py:131
  (180 shorter events, 67.4 us)
Async XLA Ops:
  23.8 13.5 %copy-start.12 = (f32[32,16]{0,1:T(8,128)S(1)}, f32[32,16]{0,1:T(8,128)}, u32[]{:S(2)}) copy-start(f32[32,16]{0,1:T(8,128)} %param.25) | copy-start | bytes 6148
  23.8 13.5 %copy-start.23 = (f32[32,16]{0,1:T(8,128)S(1)}, f32[32,16]{0,1:T(8,128)}, u32[]{:S(2)}) copy-start(f32[32,16]{0,1:T(8,128)} %param.26) | copy-start | bytes 6148
  23.8 27.7 %all-to-all-start = ((bf16[16,2,24576]{2,1,0:T(2,128)(2,1)}), bf16[16,2,24576]{2,1,0:T(2,128)(2,1)}, u32[]{:S(2)}, u32[]{:S(2)}) async-start(bf16[16,2,24576]{2,1,0:T(2,128)(2,1)} %reshape.234), calls=%async_computation | async-start | bytes 3145728 | tf_op jit(solution)/shard_map/all_to_all | solution.py:83
  29.4 53.6 %copy-start.37 = (s32[512]{0:T(512)}, s32[512]{0:T(512)S(1)}, u32[]{:S(2)}) copy-start(s32[512]{0:T(512)S(1)} %get-tuple-element.236) | copy-start | bytes 6148
  29.4 55.5 %copy-start.35 = (s32[512]{0:T(512)}, s32[512]{0:T(512)S(1)}, u32[]{:S(2)}) copy-start(s32[512]{0:T(512)S(1)} %get-tuple-element.237) | copy-start | bytes 6148
  29.4 57.3 %copy-start.33 = (s32[512]{0:T(512)}, s32[512]{0:T(512)S(1)}, u32[]{:S(2)}) copy-start(s32[512]{0:T(512)S(1)} %get-tuple-element.230) | copy-start | bytes 6148
  29.4 59.2 %copy-start.31 = (s32[512]{0:T(512)}, s32[512]{0:T(512)S(1)}, u32[]{:S(2)}) copy-start(s32[512]{0:T(512)S(1)} %get-tuple-element.231) | copy-start | bytes 6148
  29.4 61.0 %copy-start.29 = (s32[512]{0:T(512)}, s32[512]{0:T(512)S(1)}, u32[]{:S(2)}) copy-start(s32[512]{0:T(512)S(1)} %get-tuple-element.232) | copy-start | bytes 6148
  29.4 62.9 %copy-start.27 = (s32[512]{0:T(512)}, s32[512]{0:T(512)S(1)}, u32[]{:S(2)}) copy-start(s32[512]{0:T(512)S(1)} %get-tuple-element.233) | copy-start | bytes 6148
  29.4 64.7 %copy-start.25 = (s32[512]{0:T(512)}, s32[512]{0:T(512)S(1)}, u32[]{:S(2)}) copy-start(s32[512]{0:T(512)S(1)} %get-tuple-element.234) | copy-start | bytes 6148
  29.4 66.6 %copy-start.24 = (s32[512]{0:T(512)}, s32[512]{0:T(512)S(1)}, u32[]{:S(2)}) copy-start(s32[512]{0:T(512)S(1)} %get-tuple-element.229) | copy-start | bytes 6148
  64.1 39.2 %copy-start.40 = (pred[512]{0:T(512)(128)(4,1)S(1)}, pred[512]{0:T(512)(128)(4,1)}, u32[]{:S(2)}) copy-start(pred[512]{0:T(512)(128)(4,1)} %get-tuple-element.258) | copy-start | bytes 1540
  76.6 26.6 %collective-permute-start = (bf16[3,2,512]{2,1,0:T(2,128)(2,1)S(1)}, bf16[3,2,512]{2,1,0:T(2,128)(2,1)S(1)}, u32[]{:S(2)}, u32[]{:S(2)}) collective-permute-start(bf16[3,2,512]{2,1,0:T(2,128)(2,1)S(1)} %slice.154), channel_id=1, source_target_pairs={{0,16},{16,32},{32,48},{48,64},{64,80},{80,96},{96,112},{112,128},... | collective-permute-start | bytes 18440 | tf_op jit(solution)/shard_map/ppermute | solution.py:15
  110.8 43.4 %collective-permute-start.8 = (bf16[512,512]{1,0:T(8,128)(2,1)}, bf16[512,512]{1,0:T(8,128)(2,1)}, u32[]{:S(2)}, u32[]{:S(2)}) collective-permute-start(bf16[512,512]{1,0:T(8,128)(2,1)} %fusion.68), channel_id=1, source_target_pairs={{0,128},{16,144},{32,160},{48,176},{64,192},{80,208},{96,224},{112... | collective-permute-start | bytes 1572872 | tf_op jit(solution)/shard_map/ppermute | solution.py:15
  125.7 146.4 %collective-permute-start.7 = (bf16[512,512]{1,0:T(8,128)(2,1)}, bf16[512,512]{1,0:T(8,128)(2,1)}, u32[]{:S(2)}, u32[]{:S(2)}) collective-permute-start(bf16[512,512]{1,0:T(8,128)(2,1)} %fusion.68), channel_id=1, source_target_pairs={{0,112},{16,128},{32,144},{48,160},{64,176},{80,192},{96,208},{112... | collective-permute-start | bytes 1572872 | tf_op jit(solution)/shard_map/ppermute | solution.py:15
  129.7 219.2 %collective-permute-start.6 = (bf16[512,512]{1,0:T(8,128)(2,1)}, bf16[512,512]{1,0:T(8,128)(2,1)}, u32[]{:S(2)}, u32[]{:S(2)}) collective-permute-start(bf16[512,512]{1,0:T(8,128)(2,1)} %fusion.68), channel_id=1, source_target_pairs={{0,96},{16,112},{32,128},{48,144},{64,160},{80,176},{96,192},{112,... | collective-permute-start | bytes 1572872 | tf_op jit(solution)/shard_map/ppermute | solution.py:15
  132.8 226.8 %collective-permute-start.5 = (bf16[512,512]{1,0:T(8,128)(2,1)}, bf16[512,512]{1,0:T(8,128)(2,1)}, u32[]{:S(2)}, u32[]{:S(2)}) collective-permute-start(bf16[512,512]{1,0:T(8,128)(2,1)} %fusion.68), channel_id=1, source_target_pairs={{0,80},{16,96},{32,112},{48,128},{64,144},{80,160},{96,176},{112,1... | collective-permute-start | bytes 1572872 | tf_op jit(solution)/shard_map/ppermute | solution.py:15
  134.7 301.4 %collective-permute-start.4 = (bf16[512,512]{1,0:T(8,128)(2,1)}, bf16[512,512]{1,0:T(8,128)(2,1)}, u32[]{:S(2)}, u32[]{:S(2)}) collective-permute-start(bf16[512,512]{1,0:T(8,128)(2,1)} %fusion.68), channel_id=1, source_target_pairs={{0,64},{16,80},{32,96},{48,112},{64,128},{80,144},{96,160},{112,17... | collective-permute-start | bytes 1572872 | tf_op jit(solution)/shard_map/ppermute | solution.py:15
  151.2 199.5 %copy-start.41 = (f32[128]{0:T(128)S(1)}, f32[128]{0:T(128)}, u32[]{:S(2)}) copy-start(f32[128]{0:T(128)} %get-tuple-element.274) | copy-start | bytes 1540
  151.3 199.9 %copy-start.4 = (bf16[128,512]{0,1:T(8,128)(2,1)S(1)}, bf16[128,512]{0,1:T(8,128)(2,1)}, u32[]{:S(2)}) copy-start(bf16[128,512]{0,1:T(8,128)(2,1)} %copy.105) | copy-start | bytes 393220
  154.2 199.5 %copy-start.38 = (s32[512]{0:T(512)S(1)}, s32[512]{0:T(512)}, u32[]{:S(2)}) copy-start(s32[512]{0:T(512)} %copy-done.37) | copy-start | bytes 6148
  154.2 299.2 %collective-permute-start.3 = (bf16[512,512]{1,0:T(8,128)(2,1)}, bf16[512,512]{1,0:T(8,128)(2,1)}, u32[]{:S(2)}, u32[]{:S(2)}) collective-permute-start(bf16[512,512]{1,0:T(8,128)(2,1)} %fusion.68), channel_id=1, source_target_pairs={{0,48},{16,64},{32,80},{48,96},{64,112},{80,128},{96,144},{112,160... | collective-permute-start | bytes 1572872 | tf_op jit(solution)/shard_map/ppermute | solution.py:15
  272.0 202.8 %collective-permute-start.2 = (bf16[512,512]{1,0:T(8,128)(2,1)}, bf16[512,512]{1,0:T(8,128)(2,1)}, u32[]{:S(2)}, u32[]{:S(2)}) collective-permute-start(bf16[512,512]{1,0:T(8,128)(2,1)} %fusion.68), channel_id=1, source_target_pairs={{0,32},{16,48},{32,64},{48,80},{64,96},{80,112},{96,128},{112,144}... | collective-permute-start | bytes 1572872 | tf_op jit(solution)/shard_map/ppermute | solution.py:15
  348.9 137.0 %collective-permute-start.1 = (bf16[512,512]{1,0:T(8,128)(2,1)}, bf16[512,512]{1,0:T(8,128)(2,1)}, u32[]{:S(2)}, u32[]{:S(2)}) collective-permute-start(bf16[512,512]{1,0:T(8,128)(2,1)} %fusion.68), channel_id=1, source_target_pairs={{0,16},{16,32},{32,48},{48,64},{64,80},{80,96},{96,112},{112,128},... | collective-permute-start | bytes 1572872 | tf_op jit(solution)/shard_map/ppermute | solution.py:15
  359.6 76.5 %copy-start.30 = (s32[512]{0:T(512)S(1)}, s32[512]{0:T(512)}, u32[]{:S(2)}) copy-start(s32[512]{0:T(512)} %copy-done.29) | copy-start | bytes 6148
  362.3 91.0 %copy-start.28 = (s32[512]{0:T(512)S(1)}, s32[512]{0:T(512)}, u32[]{:S(2)}) copy-start(s32[512]{0:T(512)} %copy-done.27) | copy-start | bytes 6148
  438.8 36.0 %copy-start.26 = (s32[512]{0:T(512)S(1)}, s32[512]{0:T(512)}, u32[]{:S(2)}) copy-start(s32[512]{0:T(512)} %copy-done.25) | copy-start | bytes 6148
  477.5 12.4 %copy-start.10 = (f32[16,32]{0,1:T(8,128)S(1)}, f32[16,32]{0,1:T(8,128)}, u32[]{:S(2)}) copy-start(f32[16,32]{0,1:T(8,128)} %copy-done.9) | copy-start | bytes 6148
  477.5 12.4 %copy-start.13 = (f32[16,32]{0,1:T(8,128)S(1)}, f32[16,32]{0,1:T(8,128)}, u32[]{:S(2)}) copy-start(f32[16,32]{0,1:T(8,128)} %copy.121) | copy-start | bytes 6148
  477.5 12.4 %copy-start.14 = (f32[16,32]{0,1:T(8,128)S(1)}, f32[16,32]{0,1:T(8,128)}, u32[]{:S(2)}) copy-start(f32[16,32]{0,1:T(8,128)} %copy.119) | copy-start | bytes 6148
  477.5 12.4 %copy-start.15 = (f32[16,32]{0,1:T(8,128)S(1)}, f32[16,32]{0,1:T(8,128)}, u32[]{:S(2)}) copy-start(f32[16,32]{0,1:T(8,128)} %copy.117) | copy-start | bytes 6148
  477.5 12.4 %copy-start.16 = (f32[16,32]{0,1:T(8,128)S(1)}, f32[16,32]{0,1:T(8,128)}, u32[]{:S(2)}) copy-start(f32[16,32]{0,1:T(8,128)} %copy.115) | copy-start | bytes 6148
  (22 other events, 110.5 us)
where the time goes:
time: 514 us; the launch traced here: 511 us
  waiting for transfers between devices  286 us (56%)
  local copies, waits for them, and re-layouts  81.7 us (16%)
  starting transfers between devices  67.4 us (13%)
  matrix products  29.4 us (6%)
  other arithmetic  16.7 us (3%)
  blocking collectives  14.7 us (3%)
  between operations  14.6 us (3%)
    ppermute x9, waiting for transfers between devices, shifted_2(): return lax.ppermute(block, axis, route)  280 us
    ppermute x9, starting transfers between devices, shifted_2(): return lax.ppermute(block, axis, route)  62 us
    unnamed x94, local copies, waits for them, and re-layouts  38.6 us
    dot_general x20, matrix products, contract(): jnp.einsum(pattern, left_side, right_side, precision=lax.Precision.HIGHEST)  29.4 us
    all_to_all x1, blocking collectives, local(): lax.all_to_all(payload, 'fsdp', split_axis=0, concat_axis=1, tiled=True)  14.7 us
    all_to_all x1, local copies, waits for them, and re-layouts, local(): lax.all_to_all(streams, 'fsdp', split_axis=2, concat_axis=1, tiled=True)  11.8 us
  transfers between devices with their start and end apart: 10, of which 7 were waited for; matrix products, arithmetic and copies ran while one was open for 12% of the time, Pallas kernels for 0%

commit v1 on v0

--- a/solution.py
+++ b/solution.py
@@ -80,7 +80,10 @@
     padded_marks = jnp.concatenate([jnp.full((margin,), -1, jnp.int32), segments])
     tile_start = tile_index * tile_rows
     tile_marks = lax.dynamic_slice_in_dim(segments, tile_start, tile_rows)
-    local_streams = lax.all_to_all(streams, "fsdp", split_axis=2, concat_axis=1, tiled=True)
+    local_streams = jnp.concatenate(
+        lax.all_to_all(jnp.stack(jnp.split(streams, lax.axis_size("fsdp"), axis=2)), "fsdp", 0, 0),
+        axis=1,
+    )
     before_rows = shifted_2(local_streams[:, tile_rows - margin :, :], "ctx", 1)
     before_marks = lax.dynamic_slice_in_dim(padded_marks, tile_start, margin)
     queries, gated_prod = featurize(

time: 514 us -> 489 us (0.951)
  waiting for transfers between devices: 286 us -> 207 us
  starting transfers between devices: 67.4 us -> 139 us
  local copies, waits for them, and re-layouts: 81.7 us -> 58.4 us
  blocking collectives: 14.7 us -> 20.1 us
    ppermute x9, waiting for transfers between devices: 280 us -> 201 us  [shifted_2(): return lax.ppermute(block, axis, route)]
    ppermute x9, starting transfers between devices: 62 us -> 134 us  [shifted_2(): return lax.ppermute(block, axis, route)]
    unnamed x94 -> x108, local copies, waits for them, and re-layouts: 38.6 us -> 25.8 us
    all_to_all x1, local copies, waits for them, and re-layouts: 11.8 us -> 1.51 us  [local(): lax.all_to_all(jnp.stack(jnp.split(streams, lax.axis_size('fsdp'), axis=2...]
    all_to_all x1, blocking collectives: 14.7 us -> 20.1 us  [local(): lax.all_to_all(payload, 'fsdp', split_axis=0, concat_axis=1, tiled=True)]
    another operation x8 -> x9, local copies, waits for them, and re-layouts: 8.79 us -> 10.4 us
  transfers between devices with their start and end apart: 10 -> 10, of which waited for: 7 -> 8; matrix products, arithmetic and copies ran while one was open for 12% -> 12% of each run, Pallas kernels for 0% -> 0%
where the time goes in v1:
time: 489 us; the launch traced here: 487 us
  waiting for transfers between devices  207 us (42%)
  starting transfers between devices  139 us (28%)
  local copies, waits for them, and re-layouts  58.4 us (12%)
  matrix products  28.8 us (6%)
  blocking collectives  20.1 us (4%)
  other arithmetic  17.2 us (4%)
  between operations  15.4 us (3%)
    ppermute x9, waiting for transfers between devices, shifted_2(): return lax.ppermute(block, axis, route)  201 us
    ppermute x9, starting transfers between devices, shifted_2(): return lax.ppermute(block, axis, route)  134 us
    dot_general x20, matrix products, contract(): jnp.einsum(pattern, left_side, right_side, precision=lax.Precision.HIGHEST)  28.8 us
    unnamed x108, local copies, waits for them, and re-layouts  25.8 us
    all_to_all x1, blocking collectives, local(): lax.all_to_all(payload, 'fsdp', split_axis=0, concat_axis=1, tiled=True)  20.1 us
  transfers between devices with their start and end apart: 10, of which 8 were waited for; matrix products, arithmetic and copies ran while one was open for 12% of the time, Pallas kernels for 0%

profile of v1, /device:TPU:4, one launch (start us, length us, event | category | flops | bytes accessed | tf_op | source)
XLA Modules:
  0.0 486.9 jit_solution(18244165462619225754)
XLA Ops:
  24.6 5.4 %all-to-all-start = ((bf16[16,3,32,512]{3,2,1,0:T(8,128)(2,1)}), bf16[16,3,32,512]{3,2,1,0:T(8,128)(2,1)}, u32[]{:S(2)}, u32[]{:S(2)}) async-start(bf16[16,3,32,512]{3,2,1,0:T(8,128)(2,1)} %bitcast_dynamic-update-slice_fusion), calls=%async_computation | async-start | bytes 3145728 | tf_op jit(solution)/shard_map/all_to_all | solution.py:84
  34.1 2.5 compare_convert_fusion.18
  42.5 3.7 fusion.87
  46.2 6.1 %all-to-all-done = bf16[16,3,32,512]{3,2,1,0:T(8,128)(2,1)} async-done(((bf16[16,3,32,512]{3,2,1,0:T(8,128)(2,1)}), bf16[16,3,32,512]{3,2,1,0:T(8,128)(2,1)}, u32[]{:S(2)}, u32[]{:S(2)}) %all-to-all-start) | async-done | bytes 1572896 | tf_op jit(solution)/shard_map/all_to_all | solution.py:84
  55.0 3.8 collective-permute-start
  82.2 3.8 multiply_add_fusion
  89.6 7.7 %collective-permute-start.3 = (bf16[512,512]{1,0:T(8,128)(2,1)}, bf16[512,512]{1,0:T(8,128)(2,1)}, u32[]{:S(2)}, u32[]{:S(2)}) collective-permute-start(bf16[512,512]{1,0:T(8,128)(2,1)} %fusion.68), channel_id=1, source_target_pairs={{0,48},{16,64},{32,80},{48,96},{64,112},{80,128},{96,144},{112,160... | collective-permute-start | bytes 1572872 | tf_op jit(solution)/shard_map/ppermute | solution.py:15
  97.4 9.1 %collective-permute-start.4 = (bf16[512,512]{1,0:T(8,128)(2,1)}, bf16[512,512]{1,0:T(8,128)(2,1)}, u32[]{:S(2)}, u32[]{:S(2)}) collective-permute-start(bf16[512,512]{1,0:T(8,128)(2,1)} %fusion.68), channel_id=1, source_target_pairs={{0,64},{16,80},{32,96},{48,112},{64,128},{80,144},{96,160},{112,17... | collective-permute-start | bytes 1572872 | tf_op jit(solution)/shard_map/ppermute | solution.py:15
  106.5 4.7 collective-permute-start.5
  111.2 2.8 collective-permute-start.6
  124.1 2.5 fusion.40
  129.6 2.5 fusion.34
  132.1 8.3 %collective-permute-done.3 = bf16[512,512]{1,0:T(8,128)(2,1)} collective-permute-done((bf16[512,512]{1,0:T(8,128)(2,1)}, bf16[512,512]{1,0:T(8,128)(2,1)}, u32[]{:S(2)}, u32[]{:S(2)}) %collective-permute-start.3) | collective-permute-done | bytes 524320 | tf_op jit(solution)/shard_map/ppermute | solution.py:15
  140.4 5.6 %collective-permute-start.8 = (bf16[512,512]{1,0:T(8,128)(2,1)}, bf16[512,512]{1,0:T(8,128)(2,1)}, u32[]{:S(2)}, u32[]{:S(2)}) collective-permute-start(bf16[512,512]{1,0:T(8,128)(2,1)} %fusion.68), channel_id=1, source_target_pairs={{0,128},{16,144},{32,160},{48,176},{64,192},{80,208},{96,224},{112... | collective-permute-start | bytes 1572872 | tf_op jit(solution)/shard_map/ppermute | solution.py:15
  146.0 18.1 %collective-permute-done.4 = bf16[512,512]{1,0:T(8,128)(2,1)} collective-permute-done((bf16[512,512]{1,0:T(8,128)(2,1)}, bf16[512,512]{1,0:T(8,128)(2,1)}, u32[]{:S(2)}, u32[]{:S(2)}) %collective-permute-start.4) | collective-permute-done | bytes 524320 | tf_op jit(solution)/shard_map/ppermute | solution.py:15
  164.1 26.6 %collective-permute-start.1 = (bf16[512,512]{1,0:T(8,128)(2,1)}, bf16[512,512]{1,0:T(8,128)(2,1)}, u32[]{:S(2)}, u32[]{:S(2)}) collective-permute-start(bf16[512,512]{1,0:T(8,128)(2,1)} %fusion.68), channel_id=1, source_target_pairs={{0,16},{16,32},{32,48},{48,64},{64,80},{80,96},{96,112},{112,128},... | collective-permute-start | bytes 1572872 | tf_op jit(solution)/shard_map/ppermute | solution.py:15
  190.7 48.6 %collective-permute-done.5 = bf16[512,512]{1,0:T(8,128)(2,1)} collective-permute-done((bf16[512,512]{1,0:T(8,128)(2,1)}, bf16[512,512]{1,0:T(8,128)(2,1)}, u32[]{:S(2)}, u32[]{:S(2)}) %collective-permute-start.5) | collective-permute-done | bytes 524320 | tf_op jit(solution)/shard_map/ppermute | solution.py:15
  239.3 71.5 %collective-permute-start.2 = (bf16[512,512]{1,0:T(8,128)(2,1)}, bf16[512,512]{1,0:T(8,128)(2,1)}, u32[]{:S(2)}, u32[]{:S(2)}) collective-permute-start(bf16[512,512]{1,0:T(8,128)(2,1)} %fusion.68), channel_id=1, source_target_pairs={{0,32},{16,48},{32,64},{48,80},{64,96},{80,112},{96,128},{112,144}... | collective-permute-start | bytes 1572872 | tf_op jit(solution)/shard_map/ppermute | solution.py:15
  311.2 2.5 fusion.52
  313.7 2.6 conditional.10
  316.4 2.7 conditional.11
  319.1 2.7 conditional.12
  321.8 2.7 conditional.13
  324.6 81.7 %collective-permute-done.7 = bf16[512,512]{1,0:T(8,128)(2,1)} collective-permute-done((bf16[512,512]{1,0:T(8,128)(2,1)}, bf16[512,512]{1,0:T(8,128)(2,1)}, u32[]{:S(2)}, u32[]{:S(2)}) %collective-permute-start.7) | collective-permute-done | bytes 524320 | tf_op jit(solution)/shard_map/ppermute | solution.py:15
  406.3 2.7 conditional.14
  409.0 4.5 collective-permute-done.8
  413.5 25.6 %collective-permute-done.1 = bf16[512,512]{1,0:T(8,128)(2,1)} collective-permute-done((bf16[512,512]{1,0:T(8,128)(2,1)}, bf16[512,512]{1,0:T(8,128)(2,1)}, u32[]{:S(2)}, u32[]{:S(2)}) %collective-permute-start.1) | collective-permute-done | bytes 524320 | tf_op jit(solution)/shard_map/ppermute | solution.py:15
  439.1 2.6 conditional.8
  441.7 14.6 %collective-permute-done.2 = bf16[512,512]{1,0:T(8,128)(2,1)} collective-permute-done((bf16[512,512]{1,0:T(8,128)(2,1)}, bf16[512,512]{1,0:T(8,128)(2,1)}, u32[]{:S(2)}, u32[]{:S(2)}) %collective-permute-start.2) | collective-permute-done | bytes 524320 | tf_op jit(solution)/shard_map/ppermute | solution.py:15
  456.4 4.2 conditional.9
  460.6 3.3 fusion.30
  466.0 20.1 %all_to_all.24 = bf16[16,32,512]{2,1,0:T(8,128)(2,1)S(1)} all-to-all(bf16[16,32,512]{2,1,0:T(8,128)(2,1)S(1)} %bitcast.150), channel_id=1, replica_groups=mesh['ctx'=32,'fsdp'=16] {'fsdp'}, dimensions={0} | all-to-all | bytes 1048576 | tf_op jit(solution)/shard_map/all_to_all | solution.py:134
  (195 shorter events, 85.8 us)
Async XLA Ops:
  24.6 5.5 %copy-start.12 = (s32[16384]{0:T(1024)S(1)}, s32[16384]{0:T(1024)}, u32[]{:S(2)}) copy-start(s32[16384]{0:T(1024)} %param.23) | copy-start | bytes 196612
  24.6 13.0 %copy-start.23 = (f32[3,3,512]{2,1,0:T(4,128)S(1)}, f32[3,3,512]{2,1,0:T(4,128)}, u32[]{:S(2)}) copy-start(f32[3,3,512]{2,1,0:T(4,128)} %param.24) | copy-start | bytes 55300
  24.6 13.6 %copy-start.13 = (f32[32,16]{0,1:T(8,128)S(1)}, f32[32,16]{0,1:T(8,128)}, u32[]{:S(2)}) copy-start(f32[32,16]{0,1:T(8,128)} %param.25) | copy-start | bytes 6148
  24.6 13.6 %copy-start.24 = (f32[32,16]{0,1:T(8,128)S(1)}, f32[32,16]{0,1:T(8,128)}, u32[]{:S(2)}) copy-start(f32[32,16]{0,1:T(8,128)} %param.26) | copy-start | bytes 6148
  24.6 27.7 %all-to-all-start = ((bf16[16,3,32,512]{3,2,1,0:T(8,128)(2,1)}), bf16[16,3,32,512]{3,2,1,0:T(8,128)(2,1)}, u32[]{:S(2)}, u32[]{:S(2)}) async-start(bf16[16,3,32,512]{3,2,1,0:T(8,128)(2,1)} %bitcast_dynamic-update-slice_fusion), calls=%async_computation | async-start | bytes 3145728 | tf_op jit(solution)/shard_map/all_to_all | solution.py:84
  30.2 31.1 %copy-start.38 = (s32[512]{0:T(512)}, s32[512]{0:T(512)S(1)}, u32[]{:S(2)}) copy-start(s32[512]{0:T(512)S(1)} %get-tuple-element.233) | copy-start | bytes 6148
  30.2 33.1 %copy-start.36 = (s32[512]{0:T(512)}, s32[512]{0:T(512)S(1)}, u32[]{:S(2)}) copy-start(s32[512]{0:T(512)S(1)} %get-tuple-element.232) | copy-start | bytes 6148
  30.2 35.0 %copy-start.34 = (s32[512]{0:T(512)}, s32[512]{0:T(512)S(1)}, u32[]{:S(2)}) copy-start(s32[512]{0:T(512)S(1)} %get-tuple-element.231) | copy-start | bytes 6148
  30.2 36.9 %copy-start.32 = (s32[512]{0:T(512)}, s32[512]{0:T(512)S(1)}, u32[]{:S(2)}) copy-start(s32[512]{0:T(512)S(1)} %get-tuple-element.230) | copy-start | bytes 6148
  30.2 38.8 %copy-start.30 = (s32[512]{0:T(512)}, s32[512]{0:T(512)S(1)}, u32[]{:S(2)}) copy-start(s32[512]{0:T(512)S(1)} %get-tuple-element.237) | copy-start | bytes 6148
  30.2 40.8 %copy-start.28 = (s32[512]{0:T(512)}, s32[512]{0:T(512)S(1)}, u32[]{:S(2)}) copy-start(s32[512]{0:T(512)S(1)} %get-tuple-element.236) | copy-start | bytes 6148
  30.2 42.7 %copy-start.26 = (s32[512]{0:T(512)}, s32[512]{0:T(512)S(1)}, u32[]{:S(2)}) copy-start(s32[512]{0:T(512)S(1)} %get-tuple-element.229) | copy-start | bytes 6148
  30.2 44.6 %copy-start.25 = (s32[512]{0:T(512)}, s32[512]{0:T(512)S(1)}, u32[]{:S(2)}) copy-start(s32[512]{0:T(512)S(1)} %get-tuple-element.234) | copy-start | bytes 6148
  36.7 5.8 %copy-start.22 = (f32[512]{0:T(512)}, f32[512]{0:T(512)S(1)}, u32[]{:S(2)}) copy-start(f32[512]{0:T(512)S(1)} %iota_add_fusion) | copy-start | bytes 6148
  55.0 27.2 %collective-permute-start = (bf16[3,2,512]{2,1,0:T(2,128)(2,1)S(1)}, bf16[3,2,512]{2,1,0:T(2,128)(2,1)S(1)}, u32[]{:S(2)}, u32[]{:S(2)}) collective-permute-start(bf16[3,2,512]{2,1,0:T(2,128)(2,1)S(1)} %slice.154), channel_id=1, source_target_pairs={{0,16},{16,32},{32,48},{48,64},{64,80},{80,96},{96,112},{112,128},... | collective-permute-start | bytes 18440 | tf_op jit(solution)/shard_map/ppermute | solution.py:15
  89.6 50.7 %collective-permute-start.3 = (bf16[512,512]{1,0:T(8,128)(2,1)}, bf16[512,512]{1,0:T(8,128)(2,1)}, u32[]{:S(2)}, u32[]{:S(2)}) collective-permute-start(bf16[512,512]{1,0:T(8,128)(2,1)} %fusion.68), channel_id=1, source_target_pairs={{0,48},{16,64},{32,80},{48,96},{64,112},{80,128},{96,144},{112,160... | collective-permute-start | bytes 1572872 | tf_op jit(solution)/shard_map/ppermute | solution.py:15
  97.4 66.7 %collective-permute-start.4 = (bf16[512,512]{1,0:T(8,128)(2,1)}, bf16[512,512]{1,0:T(8,128)(2,1)}, u32[]{:S(2)}, u32[]{:S(2)}) collective-permute-start(bf16[512,512]{1,0:T(8,128)(2,1)} %fusion.68), channel_id=1, source_target_pairs={{0,64},{16,80},{32,96},{48,112},{64,128},{80,144},{96,160},{112,17... | collective-permute-start | bytes 1572872 | tf_op jit(solution)/shard_map/ppermute | solution.py:15
  106.5 132.8 %collective-permute-start.5 = (bf16[512,512]{1,0:T(8,128)(2,1)}, bf16[512,512]{1,0:T(8,128)(2,1)}, u32[]{:S(2)}, u32[]{:S(2)}) collective-permute-start(bf16[512,512]{1,0:T(8,128)(2,1)} %fusion.68), channel_id=1, source_target_pairs={{0,80},{16,96},{32,112},{48,128},{64,144},{80,160},{96,176},{112,1... | collective-permute-start | bytes 1572872 | tf_op jit(solution)/shard_map/ppermute | solution.py:15
  111.2 210.6 %collective-permute-start.6 = (bf16[512,512]{1,0:T(8,128)(2,1)}, bf16[512,512]{1,0:T(8,128)(2,1)}, u32[]{:S(2)}, u32[]{:S(2)}) collective-permute-start(bf16[512,512]{1,0:T(8,128)(2,1)} %fusion.68), channel_id=1, source_target_pairs={{0,96},{16,112},{32,128},{48,144},{64,160},{80,176},{96,192},{112,... | collective-permute-start | bytes 1572872 | tf_op jit(solution)/shard_map/ppermute | solution.py:15
  114.1 292.2 %collective-permute-start.7 = (bf16[512,512]{1,0:T(8,128)(2,1)}, bf16[512,512]{1,0:T(8,128)(2,1)}, u32[]{:S(2)}, u32[]{:S(2)}) collective-permute-start(bf16[512,512]{1,0:T(8,128)(2,1)} %fusion.68), channel_id=1, source_target_pairs={{0,112},{16,128},{32,144},{48,160},{64,176},{80,192},{96,208},{112... | collective-permute-start | bytes 1572872 | tf_op jit(solution)/shard_map/ppermute | solution.py:15
  119.8 4.3 copy-start.8
  129.5 181.3 %copy-start.41 = (f32[128]{0:T(128)S(1)}, f32[128]{0:T(128)}, u32[]{:S(2)}) copy-start(f32[128]{0:T(128)} %get-tuple-element.274) | copy-start | bytes 1540
  129.6 181.7 %copy-start.5 = (bf16[128,512]{0,1:T(8,128)(2,1)S(1)}, bf16[128,512]{0,1:T(8,128)(2,1)}, u32[]{:S(2)}) copy-start(bf16[128,512]{0,1:T(8,128)(2,1)} %copy.102) | copy-start | bytes 393220
  140.4 273.1 %collective-permute-start.8 = (bf16[512,512]{1,0:T(8,128)(2,1)}, bf16[512,512]{1,0:T(8,128)(2,1)}, u32[]{:S(2)}, u32[]{:S(2)}) collective-permute-start(bf16[512,512]{1,0:T(8,128)(2,1)} %fusion.68), channel_id=1, source_target_pairs={{0,128},{16,144},{32,160},{48,176},{64,192},{80,208},{96,224},{112... | collective-permute-start | bytes 1572872 | tf_op jit(solution)/shard_map/ppermute | solution.py:15
  164.1 275.0 %collective-permute-start.1 = (bf16[512,512]{1,0:T(8,128)(2,1)}, bf16[512,512]{1,0:T(8,128)(2,1)}, u32[]{:S(2)}, u32[]{:S(2)}) collective-permute-start(bf16[512,512]{1,0:T(8,128)(2,1)} %fusion.68), channel_id=1, source_target_pairs={{0,16},{16,32},{32,48},{48,64},{64,80},{80,96},{96,112},{112,128},... | collective-permute-start | bytes 1572872 | tf_op jit(solution)/shard_map/ppermute | solution.py:15
  239.3 217.0 %collective-permute-start.2 = (bf16[512,512]{1,0:T(8,128)(2,1)}, bf16[512,512]{1,0:T(8,128)(2,1)}, u32[]{:S(2)}, u32[]{:S(2)}) collective-permute-start(bf16[512,512]{1,0:T(8,128)(2,1)} %fusion.68), channel_id=1, source_target_pairs={{0,32},{16,48},{32,64},{48,80},{64,96},{80,112},{96,128},{112,144}... | collective-permute-start | bytes 1572872 | tf_op jit(solution)/shard_map/ppermute | solution.py:15
  321.8 84.5 %copy-start.31 = (s32[512]{0:T(512)S(1)}, s32[512]{0:T(512)}, u32[]{:S(2)}) copy-start(s32[512]{0:T(512)} %copy-done.30) | copy-start | bytes 6148
  406.3 7.2 %copy-start.29 = (s32[512]{0:T(512)S(1)}, s32[512]{0:T(512)}, u32[]{:S(2)}) copy-start(s32[512]{0:T(512)} %copy-done.28) | copy-start | bytes 6148
  413.5 25.6 %copy-start.27 = (s32[512]{0:T(512)S(1)}, s32[512]{0:T(512)}, u32[]{:S(2)}) copy-start(s32[512]{0:T(512)} %copy-done.26) | copy-start | bytes 6148
  456.3 4.3 copy-start.17
  456.4 4.3 copy-start.18
  456.4 4.3 copy-start.19
  (23 other events, 64.5 us)
